TPU v7x, 32 devices: a whole 2x2x4 slice. The times are simulated.
32 devices in a mesh: rep: 2 (over x), zero: 16 (over z, y, core).
Axes of the slice: x: 2, y: 2, z: 4, core: 2. Of those that a mesh axis runs over, the one named last changes fastest.
Arguments:
- gated_input: bfloat16 [2, 2048, 4096], P('rep', 'zero'), may hold values from -6 to 6
- query_gate: bfloat16 [2, 2048, 4096], P('rep', 'zero'), may hold values from -12 to 12
- cotangent: bfloat16 [2, 2048, 4096], P('rep', 'zero'), may hold values from -8 to 8
- filters: float32 [2, 256, 128], P('rep', 'zero'), may hold values from -0.5 to 0.5
- first_moment: float32 [2, 256, 128], P('rep', 'zero'), may hold values from -0.03125 to 0.03125
- second_moment: float32 [2, 256, 128], P('rep', 'zero'), may hold values from 1e-06 to 0.0001
- step_index: int32 [1], replicated, may hold values from 0 to 999
Outputs:
- query_grad: bfloat16 [2, 2048, 4096], P('rep', 'zero')
- input_grad: bfloat16 [2, 2048, 4096], P('rep', 'zero')
- new_filters: float32 [2, 256, 128], P('rep', 'zero')
All inputs are finite; a program needn't handle non-finite values.
Results may differ from a plain program's by a relative error of at most 0.007.
Values may be sent and summed in bfloat16 or wider, within the bound.
No kernel may reach another device: no remote copies, remote signals or barrier semaphores. Data moves between devices by JAX's collectives and lax.ppermute only.
A program may use at most 256 MiB of HBM per device.

v0:
```python
from functools import partial
import jax
import jax.numpy as jnp
from jax import lax
from jax.sharding import PartitionSpec as P

CLIP_NORM = 1.0
BETA_ONE = 0.9
BETA_TWO = 0.95
LEARN_RATE = 0.05
ADAM_EPS = 1e-08


def swapped(value, axis, apart):
    mask = 2**apart
    pairs = [(source, source ^ mask) for source in range(lax.axis_size(axis))]
    return lax.ppermute(value, axis, pairs)


def passed_along(block, axis, distance):
    devices = range(lax.axis_size(axis))
    route = [(i - distance, i) for i in devices if i - distance in devices]
    return lax.ppermute(block, axis, route)


def circulant(half_filters):
    groups_all, filter_len = half_filters.shape
    flipped = half_filters[:, ::-1]
    doubled = jnp.concatenate([flipped, flipped], axis=1)
    tiled = jnp.tile(doubled, (1, filter_len))
    trimmed = tiled[:, : filter_len * (2 * filter_len - 1)]
    return trimmed.reshape(groups_all, filter_len, 2 * filter_len - 1)[:, :, filter_len - 1 :]


def blocked(rows_major, groups_all, filter_len):
    tok_rows, channels = rows_major.shape
    return rows_major.T.reshape(
        groups_all, channels // groups_all, tok_rows // filter_len, filter_len
    )


def unblocked(blocks):
    groups_all, group_width, block_count, filter_len = blocks.shape
    return blocks.reshape(groups_all * group_width, block_count * filter_len).T


def swap_bit(values, bit_number):
    return swapped(values, "rep", bit_number)


def on_device(gated_input, query_gate, cotangent, filters, first_moment, second_moment, step_index):
    inputs = gated_input[0]
    gate_values = query_gate[0]
    upstream = cotangent[0]
    tok_rows, channels = inputs.shape
    filter_len = filters.shape[2]
    shard_len = filters.shape[1]
    half_filters = lax.all_gather(filters[0].astype(jnp.bfloat16), "zero", axis=0, tiled=True)
    groups_all = half_filters.shape[0]
    circ_table = circulant(half_filters)
    index_row = lax.broadcasted_iota(jnp.int32, (filter_len, filter_len), 0)
    index_col = lax.broadcasted_iota(jnp.int32, (filter_len, filter_len), 1)
    lower_mask = (index_row >= index_col)[None]
    zero_half = jnp.zeros((), jnp.bfloat16)
    table_cur = jnp.where(lower_mask, circ_table, zero_half)
    table_prev = jnp.where(lower_mask, zero_half, circ_table)
    upstream_wide = upstream.astype(jnp.float32)
    mixed_rows = (upstream_wide * gate_values.astype(jnp.float32)).astype(jnp.bfloat16)
    tail_rows = passed_along(inputs, "zero", 1)
    head_rows = passed_along(mixed_rows, "zero", -1)
    input_ext = jnp.concatenate([tail_rows, inputs], axis=0)
    mixed_ext = jnp.concatenate([mixed_rows, head_rows], axis=0)
    input_blocks = blocked(input_ext, groups_all, filter_len)
    mixed_blocks = blocked(mixed_ext, groups_all, filter_len)
    input_cur = input_blocks[:, :, 1:]
    input_prev = input_blocks[:, :, :-1]
    mixed_own = mixed_blocks[:, :, :-1]
    mixed_next = mixed_blocks[:, :, 1:]
    conv_out = jnp.einsum(
        "gik,gcbk->gcbi", table_cur, input_cur, preferred_element_type=jnp.float32
    )
    conv_out = conv_out + jnp.einsum(
        "gik,gcbk->gcbi", table_prev, input_prev, preferred_element_type=jnp.float32
    )
    query_grad = (upstream_wide * unblocked(conv_out)).astype(jnp.bfloat16)
    back_blocks = jnp.einsum(
        "gki,gcbk->gcbi", table_cur, mixed_own, preferred_element_type=jnp.float32
    )
    back_blocks = back_blocks + jnp.einsum(
        "gki,gcbk->gcbi", table_prev, mixed_next, preferred_element_type=jnp.float32
    )
    input_grad = unblocked(back_blocks).astype(jnp.bfloat16)
    lag_cur = jnp.einsum("gcbi,gcbk->gik", mixed_own, input_cur, preferred_element_type=jnp.float32)
    lag_prev = jnp.einsum(
        "gcbi,gcbk->gik", mixed_own, input_prev, preferred_element_type=jnp.float32
    )
    square = filter_len * filter_len
    front_part = jnp.pad(
        jnp.where(lower_mask, lag_cur, 0.0).reshape(groups_all, square), ((0, 0), (filter_len, 0))
    )
    rear_part = jnp.pad(
        jnp.where(lower_mask, 0.0, lag_prev).reshape(groups_all, square), ((0, 0), (0, filter_len))
    )
    skewed = (front_part + rear_part).reshape(groups_all, filter_len, filter_len + 1).sum(axis=1)
    local_grad = skewed[:, 1:][:, ::-1]
    grad_full = lax.psum(local_grad.astype(jnp.bfloat16), "zero").astype(jnp.float32)
    total_sq = jnp.sum(grad_full * grad_full)
    grad_shard = lax.dynamic_slice_in_dim(
        grad_full, lax.axis_index("zero") * shard_len, shard_len, 0
    )
    clip_scale = jnp.minimum(1.0, CLIP_NORM / (jnp.sqrt(total_sq) + 1e-06))
    clipped = grad_shard * clip_scale
    step_count = step_index[0].astype(jnp.float32) + 1.0
    moment_one = BETA_ONE * first_moment[0] + (1.0 - BETA_ONE) * clipped
    moment_two = BETA_TWO * second_moment[0] + (1.0 - BETA_TWO) * clipped * clipped
    corrected_one = moment_one / (1.0 - jnp.power(BETA_ONE, step_count))
    corrected_two = moment_two / (1.0 - jnp.power(BETA_TWO, step_count))
    stepped = filters[0] - LEARN_RATE * corrected_one / (jnp.sqrt(corrected_two) + ADAM_EPS)
    bit_count = lax.axis_size("rep").bit_length() - 1
    partner_bit = step_index[0] % bit_count
    branches = [partial(swap_bit, bit_number=number) for number in range(bit_count)]
    partner_values = lax.switch(partner_bit, branches, stepped)
    new_filters = 0.5 * (stepped + partner_values)
    return (query_grad[None], input_grad[None], new_filters[None])


def solution(mesh):
    return jax.shard_map(
        on_device,
        mesh=mesh,
        in_specs=(
            P("rep", "zero", None),
            P("rep", "zero", None),
            P("rep", "zero", None),
            P("rep", "zero", None),
            P("rep", "zero", None),
            P("rep", "zero", None),
            P(),
        ),
        out_specs=(P("rep", "zero", None), P("rep", "zero", None), P("rep", "zero", None)),
        check_vma=False,
    )
```

profile of v0, /device:TPU:8, one launch (start us, length us, event | category | flops | bytes accessed | tf_op | source)
XLA Modules:
  0.0 408.8 jit_solution(13536019468429333070)
XLA Ops:
  7.2 0.0 all-reduce.4.cloned.1.call-start
  7.2 1.9 collective-permute-start
  9.1 0.7 bitcast_convert_fusion
  9.8 23.5 %all_gather.3 = bf16[256,128]{1,0:T(8,128)(2,1)S(1)} all-gather(bf16[16,128]{1,0:T(8,128)(2,1)S(1)} %bitcast_convert_fusion), channel_id=1, replica_groups=mesh['rep'=2,'zero'=16] {'zero'}, dimensions={0}, use_global_device_ids=true | all-gather | bytes 69632 | tf_op jit(solution)/shard_map/all_gather | solution.py:58
  33.3 0.2 rev.6
  33.5 1.3 tile.4
  34.8 41.7 %copy.70 = bf16[32,8,128,256]{3,1,2,0:T(8,128)(2,1)S(1)} copy(bf16[32,8,128,256]{3,2,1,0:T(8,128)(2,1)S(1)} %bitcast.64) | data formatting | bytes 33554432
  76.5 6.6 %slice.29 = bf16[256,32640]{1,0:T(8,128)(2,1)} slice(bf16[256,32768]{1,0:T(8,128)(2,1)S(1)} %bitcast.65), slice={[0:256], [0:32640]} | slice | bytes 33423360 | tf_op jit(solution)/shard_map/slice | solution.py:31
  83.1 56.8 %reshape.85 = bf16[256,128,255]{2,1,0:T(8,128)(2,1)} reshape(bf16[256,32640]{1,0:T(8,128)(2,1)} %slice.29) | data formatting | bytes 33423360 | tf_op jit(solution)/shard_map/reshape | solution.py:32
  140.0 0.0 collective-permute-done
  140.0 0.0 copy-done.6
  140.0 1.4 maximum_bitcast_fusion
  141.4 2.5 copy.52
  143.9 2.5 reshape.83
  146.4 3.0 fusion.25
  149.4 9.6 %fusion.1 = f32[256,16,128]{2,1,0:T(8,128)S(1)} fusion(pred[128,128]{1,0:T(8,128)(4,1)S(1)} %iota_compare_fusion, bf16[256,128,255]{2,1,0:T(8,128)(2,1)} %reshape.85, bf16[256,16,1,128]{3,2,1,0:T(2,128)(2,1)S(1)} %get-tuple-element.12), kind=kOutput, calls=%fused_computation.6 | convolution fusion | flops 138412032 | bytes 11550720 | tf_op jit(solution)/shard_map/gik,gcbk->gcbi/dot_general | solution.py:79
  159.1 0.0 copy-done.4
  159.1 11.7 %fusion.10 = f32[256,16,128]{2,1,0:T(8,128)} fusion(f32[256,16,128]{2,1,0:T(8,128)S(1)} %fusion.1, pred[128,128]{1,0:T(8,128)(4,1)S(1)} %iota_compare_fusion, bf16[256,128,255]{2,1,0:T(8,128)(2,1)} %reshape.85, bf16[256,16,1,128]{3,2,1,0:T(2,128)(2,1)S(1)} %get-tuple-element.11), kind=kOutput, calls=%fused_computation.20 | convolution fusion | flops 138936320 | bytes 13647872 | tf_op jit(solution)/shard_map/gik,gcbk->gcbi/dot_general | solution.py:82
  170.8 2.1 copy.55
  172.9 3.0 fusion.9
  175.9 3.7 collective-permute-start.1
  180.3 11.6 %collective-permute-done.1 = bf16[128,4096]{1,0:T(8,128)(2,1)} collective-permute-done((bf16[128,4096]{1,0:T(8,128)(2,1)S(1)}, bf16[128,4096]{1,0:T(8,128)(2,1)}, u32[]{:S(2)}, u32[]{:S(2)}) %collective-permute-start.1) | collective-permute-done | bytes 1048608 | tf_op jit(solution)/shard_map/ppermute | solution.py:23
  191.9 1.4 maximum_bitcast_fusion.1
  193.3 2.5 copy.56
  195.8 2.5 reshape.88
  198.3 3.8 fusion.24
  202.1 7.2 %convolution_select_fusion = f32[256,128,128]{2,1,0:T(8,128)} fusion(pred[128,128]{1,0:T(8,128)(4,1)S(1)} %iota_compare_fusion, bf16[256,16,1,128]{3,2,1,0:T(2,128)(2,1)S(1)} %copy-done.5, bf16[256,16,1,128]{3,2,1,0:T(2,128)(2,1)S(1)} %get-tuple-element.10), kind=kOutput, calls=%fused_computation.1 | convolution fusion | flops 138412032 | bytes 18890752 | tf_op jit(solution)/shard_map/gcbi,gcbk->gik/dot_general | solution.py:94
  209.3 7.1 %convolution_select_fusion.1 = f32[256,128,128]{2,1,0:T(8,128)} fusion(pred[128,128]{1,0:T(8,128)(4,1)S(1)} %iota_compare_fusion, bf16[256,16,1,128]{3,2,1,0:T(2,128)(2,1)S(1)} %copy-done.3, bf16[256,16,1,128]{3,2,1,0:T(2,128)(2,1)S(1)} %get-tuple-element.10), kind=kOutput, calls=%fused_computation.2 | convolution fusion | flops 138412032 | bytes 18890752 | tf_op jit(solution)/shard_map/gcbi,gcbk->gik/dot_general | solution.py:93
  216.4 17.7 %copy.64 = f32[256,128,128]{0,2,1:T(8,128)} copy(f32[256,128,128]{2,1,0:T(8,128)} %convolution_select_fusion) | data formatting | bytes 33554432 | tf_op jit(solution)/shard_map/reshape | solution.py:102
  234.1 17.7 %copy.63 = f32[256,128,128]{0,2,1:T(8,128)} copy(f32[256,128,128]{2,1,0:T(8,128)} %convolution_select_fusion.1) | data formatting | bytes 33554432 | tf_op jit(solution)/shard_map/reshape | solution.py:99
  251.9 18.0 %pad_add_fusion = f32[256,16512]{0,1:T(8,128)} fusion(f32[256,16384]{0,1:T(8,128)} %bitcast.62, f32[256,16384]{0,1:T(8,128)} %bitcast.63), kind=kLoop, calls=%fused_computation | loop fusion | flops 4227072 | bytes 50462720 | tf_op jit(solution)/shard_map/add | solution.py:104
  269.9 18.0 %reshape.93 = f32[256,128,129]{0,2,1:T(8,128)} reshape(f32[256,16512]{0,1:T(8,128)} %pad_add_fusion) | data formatting | bytes 33816576 | tf_op jit(solution)/shard_map/reshape | solution.py:104
  287.9 7.3 %reduce_sum.18 = bf16[256,129]{0,1:T(8,128)(2,1)S(1)} reduce(f32[256,128,129]{0,2,1:T(8,128)} %reshape.93, f32[]{:T(128)} %constant.9.clone.1), dimensions={1}, to_apply=%region_0.1 | reduce | flops 4194048 | bytes 16974340 | tf_op jit(solution)/shard_map/reduce_sum | solution.py:104
  295.2 0.1 copy.69
  295.3 0.8 rev.7
  296.1 0.0 all-reduce.4.cloned.1.call-update
  296.1 0.0 copy-start.7
  296.2 0.0 copy-start.8
  296.2 0.0 copy-start.9
  296.2 10.4 %fusion = f32[256,16,128]{2,1,0:T(8,128)} fusion(pred[128,128]{1,0:T(8,128)(4,1)S(1)} %iota_compare_fusion, bf16[256,128,255]{2,1,0:T(8,128)(2,1)} %reshape.85, bf16[256,16,1,128]{3,2,1,0:T(2,128)(2,1)S(1)} %copy-done.1), kind=kOutput, calls=%fused_computation.5 | convolution fusion | flops 138412032 | bytes 11550720 | tf_op jit(solution)/shard_map/gki,gcbk->gcbi/dot_general | solution.py:86
  306.5 78.4 %all-reduce.4.cloned.1.call-done = bf16[256,128]{1,0:T(8,128)(2,1)} async-done(((bf16[256,128]{1,0:T(8,128)(2,1)}), bf16[256,128]{1,0:T(8,128)(2,1)}) %all-reduce.4.cloned.1.call-update) | async-done | bytes 65552 | tf_op jit(solution)/shard_map/psum | solution.py:106
  385.0 1.5 multiply_reduce_fusion
  387.2 0.9 convert_element_type.55
  388.1 1.5 collective-permute-start.2
  389.6 10.4 %add_convert_fusion = bf16[256,16,128]{2,1,0:T(8,128)(2,1)S(1)} fusion(f32[256,16,128]{2,1,0:T(8,128)} %fusion, pred[128,128]{1,0:T(8,128)(4,1)S(1)} %iota_compare_fusion, bf16[256,128,255]{2,1,0:T(8,128)(2,1)} %reshape.85, bf16[256,16,1,128]{3,2,1,0:T(2,128)(2,1)} %get-tuple-element.9), kind=kOutput, calls=%fused_computation.19 | convolution fusion | flops 139460608 | bytes 13647872 | tf_op jit(solution)/shard_map/gki,gcbk->gcbi/dot_general | solution.py:89
  400.0 1.3 copy.59
  401.3 0.0 collective-permute-done.2
  401.3 0.6 multiply_bitcast_fusion
  (19 shorter events, 0.1 us)
Async XLA Ops:
  7.2 377.8 %all-reduce.4.cloned.1.call-start = ((), (), s32[]{:S(2)}) async-start(), calls=%async_computation | async-start | bytes 131072 | tf_op jit(solution)/shard_map/psum | solution.py:106
  7.2 132.8 %collective-permute-start = (bf16[128,4096]{1,0:T(8,128)(2,1)}, bf16[128,4096]{1,0:T(8,128)(2,1)}, u32[]{:S(2)}, u32[]{:S(2)}) collective-permute-start(bf16[128,4096]{1,0:T(8,128)(2,1)} %bitcast.69), channel_id=1, source_target_pairs={{0,1},{1,2},{2,3},{3,4},{4,5},{5,6},{6,7},{7,8},{8,9},{9,10},{10,1... | collective-permute-start | bytes 3145736 | tf_op jit(solution)/shard_map/ppermute | solution.py:23
  83.1 56.8 %copy-start.6 = (bf16[1,128,4096]{2,1,0:T(8,128)(2,1)S(1)}, bf16[1,128,4096]{2,1,0:T(8,128)(2,1)}, u32[]{:S(2)}) copy-start(bf16[1,128,4096]{2,1,0:T(8,128)(2,1)} %param.7) | copy-start | bytes 3145732
  149.4 9.7 %copy-start.2 = (bf16[256,16,1,128]{3,2,1,0:T(2,128)(2,1)}, bf16[256,16,1,128]{3,2,1,0:T(2,128)(2,1)S(1)}, u32[]{:S(2)}) copy-start(bf16[256,16,1,128]{3,2,1,0:T(2,128)(2,1)S(1)} %get-tuple-element.12) | copy-start | bytes 3145732
  149.4 9.7 %copy-start.4 = (bf16[256,16,1,128]{3,2,1,0:T(2,128)(2,1)}, bf16[256,16,1,128]{3,2,1,0:T(2,128)(2,1)S(1)}, u32[]{:S(2)}) copy-start(bf16[256,16,1,128]{3,2,1,0:T(2,128)(2,1)S(1)} %get-tuple-element.11) | copy-start | bytes 3145732
  175.9 16.0 %collective-permute-start.1 = (bf16[128,4096]{1,0:T(8,128)(2,1)S(1)}, bf16[128,4096]{1,0:T(8,128)(2,1)}, u32[]{:S(2)}, u32[]{:S(2)}) collective-permute-start(bf16[128,4096]{1,0:T(8,128)(2,1)S(1)} %get-tuple-element.13), channel_id=1, source_target_pairs={{1,0},{2,1},{3,2},{4,3},{5,4},{6,5},{7,6},{8,7},{9,8},{10,9},{11,1... | collective-permute-start | bytes 3145736 | tf_op jit(solution)/shard_map/ppermute | solution.py:23
  198.3 3.8 copy-start.5
  202.1 7.2 %copy-start = (bf16[256,16,1,128]{3,2,1,0:T(2,128)(2,1)}, bf16[256,16,1,128]{3,2,1,0:T(2,128)(2,1)S(1)}, u32[]{:S(2)}) copy-start(bf16[256,16,1,128]{3,2,1,0:T(2,128)(2,1)S(1)} %get-tuple-element.10) | copy-start | bytes 3145732
  202.1 7.2 %copy-start.3 = (bf16[256,16,1,128]{3,2,1,0:T(2,128)(2,1)S(1)}, bf16[256,16,1,128]{3,2,1,0:T(2,128)(2,1)}, u32[]{:S(2)}) copy-start(bf16[256,16,1,128]{3,2,1,0:T(2,128)(2,1)} %copy-done.2) | copy-start | bytes 3145732
  287.9 8.3 %copy-start.1 = (bf16[256,16,1,128]{3,2,1,0:T(2,128)(2,1)S(1)}, bf16[256,16,1,128]{3,2,1,0:T(2,128)(2,1)}, u32[]{:S(2)}) copy-start(bf16[256,16,1,128]{3,2,1,0:T(2,128)(2,1)} %copy-done) | copy-start | bytes 3145732
  296.1 91.9 %copy-start.7 = (f32[1,16,128]{2,1,0:T(8,128)S(1)}, f32[1,16,128]{2,1,0:T(8,128)}, u32[]{:S(2)}) copy-start(f32[1,16,128]{2,1,0:T(8,128)} %param.10) | copy-start | bytes 24580
  296.2 91.9 %copy-start.8 = (f32[1,16,128]{2,1,0:T(8,128)S(1)}, f32[1,16,128]{2,1,0:T(8,128)}, u32[]{:S(2)}) copy-start(f32[1,16,128]{2,1,0:T(8,128)} %param.12) | copy-start | bytes 24580
  296.2 91.9 %copy-start.9 = (f32[1,16,128]{2,1,0:T(8,128)S(1)}, f32[1,16,128]{2,1,0:T(8,128)}, u32[]{:S(2)}) copy-start(f32[1,16,128]{2,1,0:T(8,128)} %param.11) | copy-start | bytes 24580
  388.1 13.2 %collective-permute-start.2 = (f32[16,128]{1,0:T(8,128)S(1)}, f32[16,128]{1,0:T(8,128)S(1)}, u32[]{:S(2)}, u32[]{:S(2)}) collective-permute-start(f32[16,128]{1,0:T(8,128)S(1)} %fusion.17), channel_id=1, source_target_pairs={{0,16},{16,0},{1,17},{17,1},{2,18},{18,2},{3,19},{19,3},{4,20},{20... | collective-permute-start | bytes 24584 | tf_op jit(solution)/shard_map/ppermute | solution.py:17
Sparse Core Ops, SparseCore 0:
  296.3 88.6 all-reduce.3
where the time goes:
time: 410 us; the launch traced here: 409 us
  local copies, waits for them, and re-layouts  181 us (44%)
  waiting for transfers between devices  90 us (22%)
  matrix products  56.3 us (14%)
  other arithmetic  34.8 us (8%)
  blocking collectives  23.5 us (6%)
  between operations  15.7 us (4%)
  starting transfers between devices  7.19 us (2%)
    psum x1, waiting for transfers between devices, on_device(): lax.psum(local_grad.astype(jnp.bfloat16), 'zero').astype(jnp.float32)  78.4 us
    reshape x1, local copies, waits for them, and re-layouts, circulant(): trimmed.reshape(groups_all, filter_len, 2 * filter_len - 1)  56.8 us
    unnamed x22, local copies, waits for them, and re-layouts  41.9 us
    all_gather x1, blocking collectives, on_device(): lax.all_gather(filters[0].astype(jnp.bfloat16), 'zero', axis=0, tiled=True)  23.5 us
    add x1, other arithmetic, on_device(): front_part + rear_part  18 us
    reshape x1, local copies, waits for them, and re-layouts, on_device(): (front_part + rear_part).reshape(groups_all, filter_len, filter_len + 1)  18 us
    reshape x1, local copies, waits for them, and re-layouts, on_device(): jnp.where(lower_mask, 0.0, lag_prev).reshape(groups_all, square)  17.7 us
    reshape x1, local copies, waits for them, and re-layouts, on_device(): jnp.where(lower_mask, lag_cur, 0.0).reshape(groups_all, square)  17.7 us
  transfers between devices with their start and end apart: 4, of which 2 were waited for; matrix products, arithmetic and copies ran while one was open for 32% of the time, Pallas kernels for 0%

commit v1 on v0

--- a/solution.py
+++ b/solution.py
@@ -55,7 +55,12 @@
     tok_rows, channels = inputs.shape
     filter_len = filters.shape[2]
     shard_len = filters.shape[1]
-    half_filters = lax.all_gather(filters[0].astype(jnp.bfloat16), "zero", axis=0, tiled=True)
+    half_filters = jnp.concatenate(
+        lax.all_to_all(
+            jnp.stack([filters[0].astype(jnp.bfloat16)] * lax.axis_size("zero")), "zero", 0, 0
+        ),
+        axis=0,
+    )
     groups_all = half_filters.shape[0]
     circ_table = circulant(half_filters)
     index_row = lax.broadcasted_iota(jnp.int32, (filter_len, filter_len), 0)

time: 410 us -> 403 us (0.983)
  blocking collectives: 23.5 us -> 0 us
  waiting for transfers between devices: 90 us -> 100 us
  starting transfers between devices: 7.19 us -> 12 us
    all_gather x1 -> x0, blocking collectives: 23.5 us -> none  [on_device(): lax.all_gather(filters[0].astype(jnp.bfloat16), 'zero', axis=0, tiled=True)]
    all_to_all x0 -> x1, waiting for transfers between devices: none -> 8.32 us  [on_device(): lax.all_to_all(jnp.stack([filters[0].astype(jnp.bfloat16)] * lax.axis_siz...]
    all_to_all x0 -> x1, starting transfers between devices: none -> 6.57 us  [on_device(): lax.all_to_all(jnp.stack([filters[0].astype(jnp.bfloat16)] * lax.axis_siz...]
  transfers between devices with their start and end apart: 4 -> 5, of which waited for: 2 -> 3; matrix products, arithmetic and copies ran while one was open for 32% -> 32% of each run, Pallas kernels for 0% -> 0%
where the time goes in v1:
time: 403 us; the launch traced here: 401 us
  local copies, waits for them, and re-layouts  182 us (45%)
  waiting for transfers between devices  100 us (25%)
  matrix products  56.3 us (14%)
  other arithmetic  34.8 us (9%)
  between operations  15.7 us (4%)
  starting transfers between devices  12 us (3%)
    psum x1, waiting for transfers between devices, on_device(): lax.psum(local_grad.astype(jnp.bfloat16), 'zero').astype(jnp.float32)  80.4 us
    reshape x1, local copies, waits for them, and re-layouts, circulant(): trimmed.reshape(groups_all, filter_len, 2 * filter_len - 1)  56.8 us
    unnamed x22, local copies, waits for them, and re-layouts  41.9 us
    reshape x1, local copies, waits for them, and re-layouts, on_device(): (front_part + rear_part).reshape(groups_all, filter_len, filter_len + 1)  18 us
    add x1, other arithmetic, on_device(): front_part + rear_part  18 us
    reshape x1, local copies, waits for them, and re-layouts, on_device(): jnp.where(lower_mask, 0.0, lag_prev).reshape(groups_all, square)  17.8 us
    reshape x1, local copies, waits for them, and re-layouts, on_device(): jnp.where(lower_mask, lag_cur, 0.0).reshape(groups_all, square)  17.7 us
    dot_general x1, matrix products, on_device(): jnp.einsum('gik,gcbk->gcbi', table_prev, input_prev, preferred_element_ty...  11.7 us
  transfers between devices with their start and end apart: 5, of which 3 were waited for; matrix products, arithmetic and copies ran while one was open for 32% of the time, Pallas kernels for 0%

profile of v1, /device:TPU:8, one launch (start us, length us, event | category | flops | bytes accessed | tf_op | source)
XLA Modules:
  0.0 401.0 jit_solution(17119948520503934421)
XLA Ops:
  7.2 1.9 collective-permute-start
  9.1 0.7 convert_bitcast_fusion
  9.8 0.6 stack.5
  10.4 6.6 %all-to-all-start = ((bf16[16,16,128]{2,1,0:T(8,128)(2,1)}), bf16[16,16,128]{2,1,0:T(8,128)(2,1)S(1)}, u32[]{:S(2)}, u32[]{:S(2)}) async-start(bf16[16,16,128]{2,1,0:T(8,128)(2,1)} %stack.5), calls=%async_computation | async-start | bytes 131072 | tf_op jit(solution)/shard_map/all_to_all | solution.py:59
  17.0 0.0 all-reduce.4.cloned.1.call-start
  17.1 8.3 %all-to-all-done = bf16[16,16,128]{2,1,0:T(8,128)(2,1)S(1)} async-done(((bf16[16,16,128]{2,1,0:T(8,128)(2,1)}), bf16[16,16,128]{2,1,0:T(8,128)(2,1)S(1)}, u32[]{:S(2)}, u32[]{:S(2)}) %all-to-all-start) | async-done | bytes 65568 | tf_op jit(solution)/shard_map/all_to_all | solution.py:59
  25.4 0.2 rev.6
  25.6 1.3 tile.4
  26.9 41.7 %copy.54 = bf16[32,8,128,256]{3,1,2,0:T(8,128)(2,1)S(1)} copy(bf16[32,8,128,256]{3,2,1,0:T(8,128)(2,1)S(1)} %bitcast.66) | data formatting | bytes 33554432
  68.6 6.7 %slice.29 = bf16[256,32640]{1,0:T(8,128)(2,1)} slice(bf16[256,32768]{1,0:T(8,128)(2,1)S(1)} %bitcast.67), slice={[0:256], [0:32640]} | slice | bytes 33423360 | tf_op jit(solution)/shard_map/slice | solution.py:31
  75.3 56.8 %reshape.90 = bf16[256,128,255]{2,1,0:T(8,128)(2,1)} reshape(bf16[256,32640]{1,0:T(8,128)(2,1)} %slice.29) | data formatting | bytes 33423360 | tf_op jit(solution)/shard_map/reshape | solution.py:32
  132.1 0.0 collective-permute-done
  132.1 1.4 maximum_bitcast_fusion
  133.5 2.5 copy.36
  136.0 2.5 reshape.87
  138.5 3.0 fusion.25
  141.5 9.6 %fusion.1 = f32[256,16,128]{2,1,0:T(8,128)S(1)} fusion(pred[128,128]{1,0:T(8,128)(4,1)S(1)} %iota_compare_fusion, bf16[256,128,255]{2,1,0:T(8,128)(2,1)} %reshape.90, bf16[256,16,1,128]{3,2,1,0:T(2,128)(2,1)S(1)} %get-tuple-element.9), kind=kOutput, calls=%fused_computation.6 | convolution fusion | flops 138412032 | bytes 11550720 | tf_op jit(solution)/shard_map/gik,gcbk->gcbi/dot_general | solution.py:84
  151.2 0.0 copy-done.4
  151.2 11.7 %fusion.10 = f32[256,16,128]{2,1,0:T(8,128)} fusion(f32[256,16,128]{2,1,0:T(8,128)S(1)} %fusion.1, pred[128,128]{1,0:T(8,128)(4,1)S(1)} %iota_compare_fusion, bf16[256,128,255]{2,1,0:T(8,128)(2,1)} %reshape.90, bf16[256,16,1,128]{3,2,1,0:T(2,128)(2,1)S(1)} %get-tuple-element.8), kind=kOutput, calls=%fused_computation.20 | convolution fusion | flops 138936320 | bytes 13647872 | tf_op jit(solution)/shard_map/gik,gcbk->gcbi/dot_general | solution.py:87
  162.8 2.1 copy.39
  164.9 3.0 fusion.9
  168.0 1.9 collective-permute-start.1
  170.6 11.6 %collective-permute-done.1 = bf16[128,4096]{1,0:T(8,128)(2,1)} collective-permute-done((bf16[128,4096]{1,0:T(8,128)(2,1)S(1)}, bf16[128,4096]{1,0:T(8,128)(2,1)}, u32[]{:S(2)}, u32[]{:S(2)}) %collective-permute-start.1) | collective-permute-done | bytes 1048608 | tf_op jit(solution)/shard_map/ppermute | solution.py:23
  182.2 1.4 maximum_bitcast_fusion.1
  183.6 2.5 copy.40
  186.0 2.5 reshape.93
  188.6 3.8 fusion.24
  192.4 7.2 %convolution_select_fusion = f32[256,128,128]{2,1,0:T(8,128)} fusion(pred[128,128]{1,0:T(8,128)(4,1)S(1)} %iota_compare_fusion, bf16[256,16,1,128]{3,2,1,0:T(2,128)(2,1)S(1)} %copy-done.5, bf16[256,16,1,128]{3,2,1,0:T(2,128)(2,1)S(1)} %get-tuple-element.7), kind=kOutput, calls=%fused_computation.1 | convolution fusion | flops 138412032 | bytes 18890752 | tf_op jit(solution)/shard_map/gcbi,gcbk->gik/dot_general | solution.py:99
  199.6 7.1 %convolution_select_fusion.1 = f32[256,128,128]{2,1,0:T(8,128)} fusion(pred[128,128]{1,0:T(8,128)(4,1)S(1)} %iota_compare_fusion, bf16[256,16,1,128]{3,2,1,0:T(2,128)(2,1)S(1)} %copy-done.3, bf16[256,16,1,128]{3,2,1,0:T(2,128)(2,1)S(1)} %get-tuple-element.7), kind=kOutput, calls=%fused_computation.2 | convolution fusion | flops 138412032 | bytes 18890752 | tf_op jit(solution)/shard_map/gcbi,gcbk->gik/dot_general | solution.py:98
  206.7 17.8 %copy.48 = f32[256,128,128]{0,2,1:T(8,128)} copy(f32[256,128,128]{2,1,0:T(8,128)} %convolution_select_fusion) | data formatting | bytes 33554432 | tf_op jit(solution)/shard_map/reshape | solution.py:107
  224.4 17.7 %copy.47 = f32[256,128,128]{0,2,1:T(8,128)} copy(f32[256,128,128]{2,1,0:T(8,128)} %convolution_select_fusion.1) | data formatting | bytes 33554432 | tf_op jit(solution)/shard_map/reshape | solution.py:104
  242.2 18.0 %pad_add_fusion = f32[256,16512]{0,1:T(8,128)} fusion(f32[256,16384]{0,1:T(8,128)} %bitcast.64, f32[256,16384]{0,1:T(8,128)} %bitcast.65), kind=kLoop, calls=%fused_computation | loop fusion | flops 4227072 | bytes 50462720 | tf_op jit(solution)/shard_map/add | solution.py:109
  260.2 18.0 %reshape.98 = f32[256,128,129]{0,2,1:T(8,128)} reshape(f32[256,16512]{0,1:T(8,128)} %pad_add_fusion) | data formatting | bytes 33816576 | tf_op jit(solution)/shard_map/reshape | solution.py:109
  278.2 7.3 %reduce_sum.18 = bf16[256,129]{0,1:T(8,128)(2,1)S(1)} reduce(f32[256,128,129]{0,2,1:T(8,128)} %reshape.98, f32[]{:T(128)} %constant.9.clone.1), dimensions={1}, to_apply=%region_0.1 | reduce | flops 4194048 | bytes 16974340 | tf_op jit(solution)/shard_map/reduce_sum | solution.py:109
  285.5 0.1 copy.53
  285.6 0.8 rev.7
  286.4 0.0 all-reduce.4.cloned.1.call-update
  286.5 0.0 copy-start.7
  286.5 0.0 copy-start.8
  286.5 0.0 copy-start.9
  286.5 10.3 %fusion = f32[256,16,128]{2,1,0:T(8,128)} fusion(pred[128,128]{1,0:T(8,128)(4,1)S(1)} %iota_compare_fusion, bf16[256,128,255]{2,1,0:T(8,128)(2,1)} %reshape.90, bf16[256,16,1,128]{3,2,1,0:T(2,128)(2,1)S(1)} %copy-done.1), kind=kOutput, calls=%fused_computation.5 | convolution fusion | flops 138412032 | bytes 11550720 | tf_op jit(solution)/shard_map/gki,gcbk->gcbi/dot_general | solution.py:91
  296.8 80.4 %all-reduce.4.cloned.1.call-done = bf16[256,128]{1,0:T(8,128)(2,1)} async-done(((bf16[256,128]{1,0:T(8,128)(2,1)}), bf16[256,128]{1,0:T(8,128)(2,1)}) %all-reduce.4.cloned.1.call-update) | async-done | bytes 65552 | tf_op jit(solution)/shard_map/psum | solution.py:111
  377.2 1.5 multiply_reduce_fusion
  379.4 0.9 convert_element_type.56
  380.3 1.5 collective-permute-start.2
  381.9 10.4 %add_convert_fusion = bf16[256,16,128]{2,1,0:T(8,128)(2,1)S(1)} fusion(f32[256,16,128]{2,1,0:T(8,128)} %fusion, pred[128,128]{1,0:T(8,128)(4,1)S(1)} %iota_compare_fusion, bf16[256,128,255]{2,1,0:T(8,128)(2,1)} %reshape.90, bf16[256,16,1,128]{3,2,1,0:T(2,128)(2,1)} %get-tuple-element.6), kind=kOutput, calls=%fused_computation.19 | convolution fusion | flops 139460608 | bytes 13647872 | tf_op jit(solution)/shard_map/gki,gcbk->gcbi/dot_general | solution.py:94
  392.2 1.3 copy.43
  393.6 0.6 multiply_bitcast_fusion
  (21 shorter events, 0.1 us)
Async XLA Ops:
  7.2 124.9 %collective-permute-start = (bf16[128,4096]{1,0:T(8,128)(2,1)}, bf16[128,4096]{1,0:T(8,128)(2,1)}, u32[]{:S(2)}, u32[]{:S(2)}) collective-permute-start(bf16[128,4096]{1,0:T(8,128)(2,1)} %bitcast.71), channel_id=1, source_target_pairs={{0,1},{1,2},{2,3},{3,4},{4,5},{5,6},{6,7},{7,8},{8,9},{9,10},{10,1... | collective-permute-start | bytes 3145736 | tf_op jit(solution)/shard_map/ppermute | solution.py:23
  10.4 15.0 %all-to-all-start = ((bf16[16,16,128]{2,1,0:T(8,128)(2,1)}), bf16[16,16,128]{2,1,0:T(8,128)(2,1)S(1)}, u32[]{:S(2)}, u32[]{:S(2)}) async-start(bf16[16,16,128]{2,1,0:T(8,128)(2,1)} %stack.5), calls=%async_computation | async-start | bytes 131072 | tf_op jit(solution)/shard_map/all_to_all | solution.py:59
  17.0 360.2 %all-reduce.4.cloned.1.call-start = ((), (), s32[]{:S(2)}) async-start(), calls=%async_computation.1 | async-start | bytes 131072 | tf_op jit(solution)/shard_map/psum | solution.py:111
  75.3 56.8 %copy-start.6 = (bf16[1,128,4096]{2,1,0:T(8,128)(2,1)S(1)}, bf16[1,128,4096]{2,1,0:T(8,128)(2,1)}, u32[]{:S(2)}) copy-start(bf16[1,128,4096]{2,1,0:T(8,128)(2,1)} %param.7) | copy-start | bytes 3145732
  141.5 9.7 %copy-start.2 = (bf16[256,16,1,128]{3,2,1,0:T(2,128)(2,1)}, bf16[256,16,1,128]{3,2,1,0:T(2,128)(2,1)S(1)}, u32[]{:S(2)}) copy-start(bf16[256,16,1,128]{3,2,1,0:T(2,128)(2,1)S(1)} %get-tuple-element.9) | copy-start | bytes 3145732
  141.5 9.7 %copy-start.4 = (bf16[256,16,1,128]{3,2,1,0:T(2,128)(2,1)}, bf16[256,16,1,128]{3,2,1,0:T(2,128)(2,1)S(1)}, u32[]{:S(2)}) copy-start(bf16[256,16,1,128]{3,2,1,0:T(2,128)(2,1)S(1)} %get-tuple-element.8) | copy-start | bytes 3145732
  168.0 14.2 %collective-permute-start.1 = (bf16[128,4096]{1,0:T(8,128)(2,1)S(1)}, bf16[128,4096]{1,0:T(8,128)(2,1)}, u32[]{:S(2)}, u32[]{:S(2)}) collective-permute-start(bf16[128,4096]{1,0:T(8,128)(2,1)S(1)} %get-tuple-element.10), channel_id=1, source_target_pairs={{1,0},{2,1},{3,2},{4,3},{5,4},{6,5},{7,6},{8,7},{9,8},{10,9},{11,1... | collective-permute-start | bytes 3145736 | tf_op jit(solution)/shard_map/ppermute | solution.py:23
  188.6 3.8 copy-start.5
  192.4 7.2 %copy-start = (bf16[256,16,1,128]{3,2,1,0:T(2,128)(2,1)}, bf16[256,16,1,128]{3,2,1,0:T(2,128)(2,1)S(1)}, u32[]{:S(2)}) copy-start(bf16[256,16,1,128]{3,2,1,0:T(2,128)(2,1)S(1)} %get-tuple-element.7) | copy-start | bytes 3145732
  192.4 7.2 %copy-start.3 = (bf16[256,16,1,128]{3,2,1,0:T(2,128)(2,1)S(1)}, bf16[256,16,1,128]{3,2,1,0:T(2,128)(2,1)}, u32[]{:S(2)}) copy-start(bf16[256,16,1,128]{3,2,1,0:T(2,128)(2,1)} %copy-done.2) | copy-start | bytes 3145732
  278.2 8.3 %copy-start.1 = (bf16[256,16,1,128]{3,2,1,0:T(2,128)(2,1)S(1)}, bf16[256,16,1,128]{3,2,1,0:T(2,128)(2,1)}, u32[]{:S(2)}) copy-start(bf16[256,16,1,128]{3,2,1,0:T(2,128)(2,1)} %copy-done) | copy-start | bytes 3145732
  286.5 93.8 %copy-start.7 = (f32[1,16,128]{2,1,0:T(8,128)S(1)}, f32[1,16,128]{2,1,0:T(8,128)}, u32[]{:S(2)}) copy-start(f32[1,16,128]{2,1,0:T(8,128)} %param.10) | copy-start | bytes 24580
  286.5 93.8 %copy-start.8 = (f32[1,16,128]{2,1,0:T(8,128)S(1)}, f32[1,16,128]{2,1,0:T(8,128)}, u32[]{:S(2)}) copy-start(f32[1,16,128]{2,1,0:T(8,128)} %param.12) | copy-start | bytes 24580
  286.5 93.8 %copy-start.9 = (f32[1,16,128]{2,1,0:T(8,128)S(1)}, f32[1,16,128]{2,1,0:T(8,128)}, u32[]{:S(2)}) copy-start(f32[1,16,128]{2,1,0:T(8,128)} %param.11) | copy-start | bytes 24580
  380.3 13.2 %collective-permute-start.2 = (f32[16,128]{1,0:T(8,128)S(1)}, f32[16,128]{1,0:T(8,128)S(1)}, u32[]{:S(2)}, u32[]{:S(2)}) collective-permute-start(f32[16,128]{1,0:T(8,128)S(1)} %fusion.17), channel_id=1, source_target_pairs={{0,16},{16,0},{1,17},{17,1},{2,18},{18,2},{3,19},{19,3},{4,20},{20... | collective-permute-start | bytes 24584 | tf_op jit(solution)/shard_map/ppermute | solution.py:17
Sparse Core Ops, SparseCore 0:
  286.6 90.6 all-reduce.3
